TPU v7x, 256 devices: a whole 4x4x8 slice. The times are simulated.
256 devices in a mesh: shift: 8 (over x, core), rows: 32 (over y, z).
Axes of the slice: x: 4, y: 4, z: 8, core: 2. Of those that a mesh axis runs over, the one named last changes fastest.
Arguments:
- neighbours: int32 [256, 8], P('rows'), may hold values from 0 to 255, as said below
- couplings: float32 [256, 8, 128, 128], P('rows'), may hold values from -0.01953125 to 0.01953125
- eigvectors: float32 [256, 128, 128], P('rows'), may hold values from -1 to 1, as said below
- eigvalues: float32 [256, 128], P('rows'), may hold values from -2.5 to 2.5
- start_block: float32 [32768, 128], P('rows'), may hold values from -240 to 240
Outputs:
- basis: float32 [32768, 128], P('rows')
- basis_image: float32 [32768, 128], P('rows')
- projected: float32 [128, 128], replicated
Inputs may be any that keep to these rules, and one draw needn't show every extreme that they name: Each block's 8 neighbours are distinct blocks other than itself, each within 8 blocks of it. `eigvectors`: each block's matrix has orthonormal columns up to rounding.
All inputs are finite; a program needn't handle non-finite values.
Results may differ from a plain program's by a relative error of at most 0.00025.
Values sent between devices are 32-bit elements; how exact they have to be, the bound alone decides.
A program may use at most 64 MiB of HBM per device.

v0:
```python
import jax
import jax.numpy as jnp
from jax import lax
from jax.sharding import PartitionSpec as P

SWEEPS = 3
radius = 1.0
damping = 0.8


def extended(block, sides, width):
    for axis, dim in sides:
        count = lax.axis_size(axis)
        forward = [(i, i + 1) for i in range(count - 1)]
        backward = [(target, source) for source, target in forward]
        low = lax.ppermute(
            lax.slice_in_dim(block, block.shape[dim] - width, None, axis=dim), axis, forward
        )
        high = lax.ppermute(lax.slice_in_dim(block, 0, width, axis=dim), axis, backward)
        block = jnp.concatenate([low, block, high], axis=dim)
    return block


def unrotate(vectors, field):
    return jnp.einsum("imn,imc->inc", vectors, field, precision=lax.Precision.HIGHEST)


def rotate(vectors, field):
    return jnp.einsum("inm,imc->inc", vectors, field, precision=lax.Precision.HIGHEST)


def shifted_inverse(vectors, values, field, real_part, imag_part):
    width = field.shape[-1] // 2
    spun = unrotate(vectors, field)
    offset = real_part - values
    denom = offset * offset + imag_part * imag_part
    scale_re = (offset / denom)[..., None]
    scale_im = (-imag_part / denom)[..., None]
    first = spun[..., :width]
    second = spun[..., width:]
    mixed = jnp.concatenate(
        [scale_re * first - scale_im * second, scale_re * second + scale_im * first], axis=-1
    )
    return rotate(vectors, mixed)


def diagonal_part(vectors, values, field):
    return rotate(vectors, values[..., None] * unrotate(vectors, field))


def coupled(near_blocks, couplings):
    return jnp.einsum("iknm,ikmc->inc", couplings, near_blocks, precision=lax.Precision.HIGHEST)


def product(left, right):
    return jnp.dot(left, right, precision=lax.Precision.HIGHEST)


def per_device(neighbours, couplings, eigvectors, eigvalues, start_block):
    blk_dev, blk = eigvalues.shape
    ncol = start_block.shape[1]
    rows_here = blk_dev * blk
    total = rows_here * lax.axis_size("rows")
    count = lax.axis_size("shift")
    angle = jnp.pi * (lax.axis_index("shift").astype(jnp.float32) + 0.5) / count
    real_part = radius * jnp.cos(angle)
    imag_part = radius * jnp.sin(angle)
    local_index = neighbours - (lax.axis_index("rows") * blk_dev - blk_dev)

    def operate_on(field, padded):
        blocks_all = padded.reshape(3 * blk_dev, blk, padded.shape[-1])
        near = blocks_all[local_index]
        return diagonal_part(eigvectors, eigvalues, field) + coupled(near, couplings)

    blocks_b = start_block.reshape(blk_dev, blk, ncol)
    rhs = jnp.concatenate([blocks_b, jnp.zeros_like(blocks_b)], axis=-1)
    iterate = damping * shifted_inverse(eigvectors, eigvalues, rhs, real_part, imag_part)
    for sweep in range(1, SWEEPS):
        first = iterate[..., :ncol]
        second = iterate[..., ncol:]
        shifted = jnp.concatenate(
            [real_part * first - imag_part * second, imag_part * first + real_part * second],
            axis=-1,
        )
        iterate_padded = extended(iterate.reshape(rows_here, 2 * ncol), (("rows", 0),), rows_here)
        resid = rhs - shifted + operate_on(iterate, iterate_padded)
        iterate = iterate + damping * shifted_inverse(
            eigvectors, eigvalues, resid, real_part, imag_part
        )
    contrib = real_part / count * iterate[..., :ncol] - imag_part / count * iterate[..., ncol:]
    contrib = contrib.reshape(rows_here, ncol)
    field = lax.psum(contrib, "shift")
    gram = lax.psum(product(field.T, field), "rows") / total
    factor = jnp.linalg.cholesky(gram)
    basis = jax.scipy.linalg.solve_triangular(factor, field.T, lower=True).T
    padded = extended(basis, (("rows", 0),), rows_here)
    image = operate_on(basis.reshape(blk_dev, blk, ncol), padded).reshape(rows_here, ncol)
    projected = lax.psum(product(basis.T, image), "rows") / total
    basis_image, projected = (image, projected)
    return (basis, basis_image, projected)


def solution(mesh):
    in_specs = (
        P("rows", None),
        P("rows", None, None, None),
        P("rows", None, None),
        P("rows", None),
        P("rows", None),
    )
    out_specs = (P("rows", None), P("rows", None), P())
    return jax.shard_map(
        per_device, mesh=mesh, in_specs=in_specs, out_specs=out_specs, check_vma=False
    )
```

profile of v0, /device:TPU:2, one launch (start us, length us, event | category | flops | bytes accessed | tf_op | source)
XLA Modules:
  0.0 556.1 jit_solution(6460307151305128019)
XLA Ops:
  12.9 4.8 collective-permute-start
  22.3 17.1 %collective-permute-done = f32[1024,256]{1,0:T(8,128)} collective-permute-done((f32[1024,256]{1,0:T(8,128)}, f32[1024,256]{1,0:T(8,128)}, u32[]{:S(2)}, u32[]{:S(2)}) %collective-permute-start) | collective-permute-done | bytes 1048608 | tf_op jit(solution)/shard_map/ppermute | solution.py:16
  39.4 5.1 collective-permute-done.1
  44.5 3.8 pad_maximum_fusion
  48.3 6.2 %gather_fusion = f32[64,128,256]{2,1,0:T(8,128)} fusion(f32[24,128,256]{2,1,0:T(8,128)} %bitcast.105, s32[1024]{0:T(1024)S(1)} %pad_clamp_fusion), kind=kCustom, calls=%fused_computation | custom fusion | bytes 16777472 | tf_op jit(solution)/shard_map/gather | solution.py:72
  54.5 17.7 %fusion.11 = f32[8,128,256]{1,2,0:T(8,128)S(1)} fusion(f32[8,256,128]{2,1,0:T(8,128)S(1)} %fusion.37, f32[8,8,128,256]{3,2,1,0:T(8,128)} %bitcast.108, f32[8,8,128,128]{3,2,1,0:T(8,128)} %param.6, f32[8,128,128]{1,2,0:T(8,128)S(1)} %copy.20, f32[8,128,128]{1,2,0:T(8,128)} %get-tuple-element.18, f32[8,128,128]{1,2,0:T(8,128)} %get-tuple-element.17), kind=kOutput, calls=%fused_computation.26 | convolution fusion | flops 3222274048 | bytes 16252928 | tf_op jit(solution)/shard_map/iknm,ikmc->inc/dot_general | solution.py:52
  75.8 4.0 collective-permute-start.2
  84.3 16.2 %collective-permute-done.2 = f32[1024,256]{1,0:T(8,128)} collective-permute-done((f32[1024,256]{1,0:T(8,128)}, f32[1024,256]{1,0:T(8,128)}, u32[]{:S(2)}, u32[]{:S(2)}) %collective-permute-start.2) | collective-permute-done | bytes 1048608 | tf_op jit(solution)/shard_map/ppermute | solution.py:16
  100.6 5.6 %collective-permute-done.3 = f32[1024,256]{1,0:T(8,128)} collective-permute-done((f32[1024,256]{1,0:T(8,128)}, f32[1024,256]{1,0:T(8,128)}, u32[]{:S(2)}, u32[]{:S(2)}) %collective-permute-start.3) | collective-permute-done | bytes 1048608 | tf_op jit(solution)/shard_map/ppermute | solution.py:19
  106.2 3.8 pad_maximum_fusion.1
  110.0 6.2 %gather_fusion.1 = f32[64,128,256]{2,1,0:T(8,128)} fusion(f32[24,128,256]{2,1,0:T(8,128)} %bitcast.106, s32[1024]{0:T(1024)S(1)} %pad_clamp_fusion), kind=kCustom, calls=%fused_computation.1 | custom fusion | bytes 16777472 | tf_op jit(solution)/shard_map/gather | solution.py:72
  116.2 17.3 %fusion.14 = f32[8,128,256]{1,2,0:T(8,128)S(1)} fusion(f32[8,256,128]{2,1,0:T(8,128)S(1)} %fusion.38, f32[8,8,128,256]{3,2,1,0:T(8,128)} %bitcast.107, f32[8,8,128,128]{3,2,1,0:T(8,128)} %param.6, f32[8,128,128]{1,2,0:T(8,128)S(1)} %copy.20, f32[8,128,128]{1,2,0:T(8,128)} %get-tuple-element.16, f32[8,128,128]{1,2,0:T(8,128)} %get-tuple-element.15), kind=kOutput, calls=%fused_computation.29 | convolution fusion | flops 3222274048 | bytes 16252928 | tf_op jit(solution)/shard_map/iknm,ikmc->inc/dot_general | solution.py:52
  137.0 65.0 %all-reduce.5.cloned.1.call-done = f32[1024,128]{1,0:T(8,128)} async-done(((f32[1024,128]{1,0:T(8,128)}), f32[1024,128]{1,0:T(8,128)}) %all-reduce.5.cloned.1.call-update) | async-done | bytes 524304 | tf_op jit(solution)/shard_map/psum | solution.py:92
  202.0 2.8 fusion.39
  205.1 143.7 %all-reduce.7.cloned.1.call-done = f32[128,128]{0,1:T(8,128)} async-done(((f32[128,128]{0,1:T(8,128)}), f32[128,128]{0,1:T(8,128)}) %all-reduce.7.cloned.1.call-update) | async-done | bytes 65552 | tf_op jit(solution)/shard_map/psum | solution.py:93
  350.5 11.7 %cholesky.16 = f32[128,128]{1,0:T(8,128)S(1)} custom-call(f32[128,128]{1,0:T(8,128)S(1)} %fusion.30), custom_call_target="Cholesky" | custom-call | tf_op jit(solution)/shard_map/jit(cholesky)/cholesky | solution.py:94
  363.6 9.8 %custom-call.7 = f32[1,128,128]{1,2,0:T(8,128)S(1)} custom-call(f32[1,128,128]{2,1,0:T(8,128)S(1)} %fusion.27), custom_call_target="InvertDiagBlocksLowerTriangular" | custom-call | tf_op jit(solution)/shard_map/jit(_solve_triangular)/triangular_solve | solution.py:95
  375.1 3.2 collective-permute-start.4
  380.5 4.7 collective-permute-done.4
  385.2 4.2 collective-permute-done.5
  390.6 1.9 copy.48
  392.5 2.8 gather_fusion.2
  395.3 8.1 %convolution_bitcast_fusion.4 = f32[8,128,128]{1,2,0:T(8,128)S(1)} fusion(f32[8,8,128,128]{3,2,1,0:T(8,128)} %bitcast.112, f32[8,8,128,128]{3,2,1,0:T(8,128)} %param.6), kind=kOutput, calls=%fused_computation.30 | convolution fusion | flops 1610612736 | bytes 8912896 | tf_op jit(solution)/shard_map/iknm,ikmc->inc/dot_general | solution.py:52
  407.2 140.5 %all-reduce.9.cloned.1.call-done = f32[128,128]{0,1:T(8,128)} async-done(((f32[128,128]{0,1:T(8,128)}), f32[128,128]{0,1:T(8,128)}) %all-reduce.9.cloned.1.call-update) | async-done | bytes 65552 | tf_op jit(solution)/shard_map/psum | solution.py:98
  (55 shorter events, 35.6 us)
Async XLA Ops:
  7.2 1.5 copy-start
  7.2 194.8 %all-reduce.5.cloned.1.call-start = ((), (), s32[]{:S(2)}) async-start(), calls=%async_computation | async-start | bytes 1048576 | tf_op jit(solution)/shard_map/psum | solution.py:92
  8.6 10.3 %copy-start.3 = (s32[8,8]{1,0:T(8,128)S(1)}, s32[8,8]{1,0:T(8,128)}, u32[]{:S(2)}) copy-start(s32[8,8]{1,0:T(8,128)} %param.5) | copy-start | bytes 772
  10.3 9.9 %copy-start.2 = (f32[8,128]{1,0:T(8,128)S(1)}, f32[8,128]{1,0:T(8,128)}, u32[]{:S(2)}) copy-start(f32[8,128]{1,0:T(8,128)} %param.8) | copy-start | bytes 12292
  12.9 26.5 %collective-permute-start = (f32[1024,256]{1,0:T(8,128)}, f32[1024,256]{1,0:T(8,128)}, u32[]{:S(2)}, u32[]{:S(2)}) collective-permute-start(f32[1024,256]{1,0:T(8,128)} %bitcast.3), channel_id=1, source_target_pairs={{0,1},{1,2},{2,3},{3,4},{4,5},{5,6},{6,7},{7,8},{8,9},{9,10},{10,1... | collective-permute-start | bytes 3145736 | tf_op jit(solution)/shard_map/ppermute | solution.py:16
  17.7 26.8 %collective-permute-start.1 = (f32[1024,256]{1,0:T(8,128)}, f32[1024,256]{1,0:T(8,128)}, u32[]{:S(2)}, u32[]{:S(2)}) collective-permute-start(f32[1024,256]{1,0:T(8,128)} %bitcast.3), channel_id=1, source_target_pairs={{1,0},{2,1},{3,2},{4,3},{5,4},{6,5},{7,6},{8,7},{9,8},{10,9},{11,1... | collective-permute-start | bytes 3145736 | tf_op jit(solution)/shard_map/ppermute | solution.py:19
  75.8 24.8 %collective-permute-start.2 = (f32[1024,256]{1,0:T(8,128)}, f32[1024,256]{1,0:T(8,128)}, u32[]{:S(2)}, u32[]{:S(2)}) collective-permute-start(f32[1024,256]{1,0:T(8,128)} %bitcast.11), channel_id=1, source_target_pairs={{0,1},{1,2},{2,3},{3,4},{4,5},{5,6},{6,7},{7,8},{8,9},{9,10},{10,1... | collective-permute-start | bytes 3145736 | tf_op jit(solution)/shard_map/ppermute | solution.py:16
  79.8 26.4 %collective-permute-start.3 = (f32[1024,256]{1,0:T(8,128)}, f32[1024,256]{1,0:T(8,128)}, u32[]{:S(2)}, u32[]{:S(2)}) collective-permute-start(f32[1024,256]{1,0:T(8,128)} %bitcast.11), channel_id=1, source_target_pairs={{1,0},{2,1},{3,2},{4,3},{5,4},{6,5},{7,6},{8,7},{9,8},{10,9},{11,1... | collective-permute-start | bytes 3145736 | tf_op jit(solution)/shard_map/ppermute | solution.py:19
  136.9 211.8 %all-reduce.7.cloned.1.call-start = ((), (), s32[]{:S(2)}) async-start(), calls=%async_computation.1 | async-start | bytes 131072 | tf_op jit(solution)/shard_map/psum | solution.py:93
  204.8 342.9 %all-reduce.9.cloned.1.call-start = ((), (), s32[]{:S(2)}) async-start(), calls=%async_computation.2 | async-start | bytes 131072 | tf_op jit(solution)/shard_map/psum | solution.py:98
  375.1 10.1 %collective-permute-start.4 = (f32[1024,128]{0,1:T(8,128)S(1)}, f32[1024,128]{0,1:T(8,128)S(1)}, u32[]{:S(2)}, u32[]{:S(2)}) collective-permute-start(f32[1024,128]{0,1:T(8,128)S(1)} %bitcast.113), channel_id=1, source_target_pairs={{0,1},{1,2},{2,3},{3,4},{4,5},{5,6},{6,7},{7,8},{8,9},{9,10},{10,1... | collective-permute-start | bytes 1572872 | tf_op jit(solution)/shard_map/ppermute | solution.py:16
  378.3 11.1 %collective-permute-start.5 = (f32[1024,128]{0,1:T(8,128)S(1)}, f32[1024,128]{0,1:T(8,128)S(1)}, u32[]{:S(2)}, u32[]{:S(2)}) collective-permute-start(f32[1024,128]{0,1:T(8,128)S(1)} %bitcast.114), channel_id=1, source_target_pairs={{1,0},{2,1},{3,2},{4,3},{5,4},{6,5},{7,6},{8,7},{9,8},{10,9},{11,1... | collective-permute-start | bytes 1572872 | tf_op jit(solution)/shard_map/ppermute | solution.py:19
  404.6 144.7 %copy-start.1 = (f32[8,128,128]{1,2,0:T(8,128)}, f32[8,128,128]{1,2,0:T(8,128)S(1)}, u32[]{:S(2)}) copy-start(f32[8,128,128]{1,2,0:T(8,128)S(1)} %convolution_add_fusion) | copy-start | bytes 1572868
Sparse Core Ops, SparseCore 0:
  137.1 64.8 all-reduce.4
  206.0 142.7 all-reduce.6
  406.4 141.3 all-reduce.8
where the time goes:
time: 562 us; the launch traced here: 556 us
  waiting for transfers between devices  402 us (72%)
  matrix products  61.7 us (11%)
  other arithmetic  37.6 us (7%)
  local copies, waits for them, and re-layouts  23.8 us (4%)
  starting transfers between devices  16.5 us (3%)
  between operations  14.5 us (3%)
    psum x1, waiting for transfers between devices, per_device(): gram = lax.psum(product(field.T, field), 'rows') / total  144 us
    psum x1, waiting for transfers between devices, per_device(): projected = lax.psum(product(basis.T, image), 'rows') / total  140 us
    psum x1, waiting for transfers between devices, per_device(): field = lax.psum(contrib, 'shift')  65 us
    dot_general x3, matrix products, coupled(): jnp.einsum('iknm,ikmc->inc', couplings, near_blocks, precision=lax.Precis...  43.1 us
    ppermute x3, waiting for transfers between devices, extended(): lax.ppermute(lax.slice_in_dim(block, block.shape[dim] - width, None, axis...  38 us
    gather x3, local copies, waits for them, and re-layouts, operate_on(): near = blocks_all[local_index]  15.2 us
    ppermute x3, waiting for transfers between devices, extended(): lax.ppermute(lax.slice_in_dim(block, 0, width, axis=dim), axis, backward)  14.9 us
    another operation x3, other arithmetic, per_device(): factor = jnp.linalg.cholesky(gram)  12.4 us
  transfers between devices with their start and end apart: 9, of which 9 were waited for; matrix products, arithmetic and copies ran while one was open for 1% of the time, Pallas kernels for 0%

commit v1 on v0

--- a/solution.py
+++ b/solution.py
@@ -89,7 +89,7 @@
         )
     contrib = real_part / count * iterate[..., :ncol] - imag_part / count * iterate[..., ncol:]
     contrib = contrib.reshape(rows_here, ncol)
-    field = lax.psum(contrib, "shift")
+    field = jnp.sum(lax.all_gather(contrib, "shift"), axis=0)
     gram = lax.psum(product(field.T, field), "rows") / total
     factor = jnp.linalg.cholesky(gram)
     basis = jax.scipy.linalg.solve_triangular(factor, field.T, lower=True).T

time: 562 us -> 530 us (0.943)
  waiting for transfers between devices: 402 us -> 370 us
    psum x1 -> x0, waiting for transfers between devices: 65 us -> none  [per_device(): field = lax.psum(contrib, 'shift')]
    all_gather x0 -> x1, waiting for transfers between devices: none -> 34.7 us  [per_device(): field = jnp.sum(lax.all_gather(contrib, 'shift'), axis=0)]
  transfers between devices with their start and end apart: 9 -> 9, of which waited for: 9 -> 9; matrix products, arithmetic and copies ran while one was open for 1% -> 2% of each run, Pallas kernels for 0% -> 0%
where the time goes in v1:
time: 530 us; the launch traced here: 525 us
  waiting for transfers between devices  370 us (70%)
  matrix products  59.4 us (11%)
  other arithmetic  40.1 us (8%)
  local copies, waits for them, and re-layouts  23.8 us (4%)
  starting transfers between devices  16.5 us (3%)
  between operations  14.5 us (3%)
    psum x1, waiting for transfers between devices, per_device(): gram = lax.psum(product(field.T, field), 'rows') / total  142 us
    psum x1, waiting for transfers between devices, per_device(): projected = lax.psum(product(basis.T, image), 'rows') / total  141 us
    dot_general x3, matrix products, coupled(): jnp.einsum('iknm,ikmc->inc', couplings, near_blocks, precision=lax.Precis...  43.1 us
    ppermute x3, waiting for transfers between devices, extended(): lax.ppermute(lax.slice_in_dim(block, block.shape[dim] - width, None, axis...  38 us
    all_gather x1, waiting for transfers between devices, per_device(): field = jnp.sum(lax.all_gather(contrib, 'shift'), axis=0)  34.7 us
    gather x3, local copies, waits for them, and re-layouts, operate_on(): near = blocks_all[local_index]  15.2 us
    ppermute x3, waiting for transfers between devices, extended(): lax.ppermute(lax.slice_in_dim(block, 0, width, axis=dim), axis, backward)  14.9 us
    another operation x3, other arithmetic, per_device(): factor = jnp.linalg.cholesky(gram)  12.4 us
  transfers between devices with their start and end apart: 9, of which 9 were waited for; matrix products, arithmetic and copies ran while one was open for 2% of the time, Pallas kernels for 0%

profile of v1, /device:TPU:2, one launch (start us, length us, event | category | flops | bytes accessed | tf_op | source)
XLA Modules:
  0.0 524.5 jit_solution(15951234211599789368)
XLA Ops:
  12.9 4.8 collective-permute-start
  22.3 17.1 %collective-permute-done = f32[1024,256]{1,0:T(8,128)} collective-permute-done((f32[1024,256]{1,0:T(8,128)}, f32[1024,256]{1,0:T(8,128)}, u32[]{:S(2)}, u32[]{:S(2)}) %collective-permute-start) | collective-permute-done | bytes 1048608 | tf_op jit(solution)/shard_map/ppermute | solution.py:16
  39.4 5.1 collective-permute-done.1
  44.5 3.8 pad_maximum_fusion
  48.3 6.2 %gather_fusion = f32[64,128,256]{2,1,0:T(8,128)} fusion(f32[24,128,256]{2,1,0:T(8,128)} %bitcast.107, s32[1024]{0:T(1024)S(1)} %pad_clamp_fusion), kind=kCustom, calls=%fused_computation | custom fusion | bytes 16777472 | tf_op jit(solution)/shard_map/gather | solution.py:72
  54.5 17.7 %fusion.11 = f32[8,128,256]{1,2,0:T(8,128)S(1)} fusion(f32[8,256,128]{2,1,0:T(8,128)S(1)} %fusion.37, f32[8,8,128,256]{3,2,1,0:T(8,128)} %bitcast.110, f32[8,8,128,128]{3,2,1,0:T(8,128)} %param.6, f32[8,128,128]{1,2,0:T(8,128)S(1)} %copy.36, f32[8,128,128]{1,2,0:T(8,128)} %get-tuple-element.21, f32[8,128,128]{1,2,0:T(8,128)} %get-tuple-element.20), kind=kOutput, calls=%fused_computation.26 | convolution fusion | flops 3222274048 | bytes 16252928 | tf_op jit(solution)/shard_map/iknm,ikmc->inc/dot_general | solution.py:52
  75.8 4.0 collective-permute-start.2
  84.3 16.2 %collective-permute-done.2 = f32[1024,256]{1,0:T(8,128)} collective-permute-done((f32[1024,256]{1,0:T(8,128)}, f32[1024,256]{1,0:T(8,128)}, u32[]{:S(2)}, u32[]{:S(2)}) %collective-permute-start.2) | collective-permute-done | bytes 1048608 | tf_op jit(solution)/shard_map/ppermute | solution.py:16
  100.6 5.6 %collective-permute-done.3 = f32[1024,256]{1,0:T(8,128)} collective-permute-done((f32[1024,256]{1,0:T(8,128)}, f32[1024,256]{1,0:T(8,128)}, u32[]{:S(2)}, u32[]{:S(2)}) %collective-permute-start.3) | collective-permute-done | bytes 1048608 | tf_op jit(solution)/shard_map/ppermute | solution.py:19
  106.2 3.8 pad_maximum_fusion.1
  110.0 6.2 %gather_fusion.1 = f32[64,128,256]{2,1,0:T(8,128)} fusion(f32[24,128,256]{2,1,0:T(8,128)} %bitcast.108, s32[1024]{0:T(1024)S(1)} %pad_clamp_fusion), kind=kCustom, calls=%fused_computation.1 | custom fusion | bytes 16777472 | tf_op jit(solution)/shard_map/gather | solution.py:72
  116.2 17.3 %fusion.14 = f32[8,128,256]{1,2,0:T(8,128)S(1)} fusion(f32[8,256,128]{2,1,0:T(8,128)S(1)} %fusion.38, f32[8,8,128,256]{3,2,1,0:T(8,128)} %bitcast.109, f32[8,8,128,128]{3,2,1,0:T(8,128)} %param.6, f32[8,128,128]{1,2,0:T(8,128)S(1)} %copy.36, f32[8,128,128]{1,2,0:T(8,128)} %get-tuple-element.19, f32[8,128,128]{1,2,0:T(8,128)} %get-tuple-element.18), kind=kOutput, calls=%fused_computation.29 | convolution fusion | flops 3222274048 | bytes 16252928 | tf_op jit(solution)/shard_map/iknm,ikmc->inc/dot_general | solution.py:52
  137.0 34.7 %all-gather.2.cloned.1.call-done = f32[8,1024,128]{2,1,0:T(8,128)} async-done(((f32[1,1024,128]{2,1,0:T(8,128)}), f32[8,1024,128]{2,1,0:T(8,128)}) %all-gather.2.cloned.1.call-update) | async-done | bytes 4194320 | tf_op jit(solution)/shard_map/all_gather | solution.py:92
  171.7 2.4 reduce_sum.9
  176.0 142.1 %all-reduce.4.cloned.1.call-done = f32[128,128]{0,1:T(8,128)} async-done(((f32[128,128]{0,1:T(8,128)}), f32[128,128]{0,1:T(8,128)}) %all-reduce.4.cloned.1.call-update) | async-done | bytes 65552 | tf_op jit(solution)/shard_map/psum | solution.py:93
  320.0 11.7 %cholesky.16 = f32[128,128]{1,0:T(8,128)S(1)} custom-call(f32[128,128]{1,0:T(8,128)S(1)} %fusion.30), custom_call_target="Cholesky" | custom-call | tf_op jit(solution)/shard_map/jit(cholesky)/cholesky | solution.py:94
  333.0 9.8 %custom-call.7 = f32[1,128,128]{1,2,0:T(8,128)S(1)} custom-call(f32[1,128,128]{2,1,0:T(8,128)S(1)} %fusion.27), custom_call_target="InvertDiagBlocksLowerTriangular" | custom-call | tf_op jit(solution)/shard_map/jit(_solve_triangular)/triangular_solve | solution.py:95
  343.5 3.2 collective-permute-start.4
  348.9 4.7 collective-permute-done.4
  353.6 4.2 collective-permute-done.5
  359.0 1.9 copy.66
  360.9 2.8 gather_fusion.2
  363.7 8.1 %convolution_bitcast_fusion.4 = f32[8,128,128]{1,2,0:T(8,128)S(1)} fusion(f32[8,8,128,128]{3,2,1,0:T(8,128)} %bitcast.114, f32[8,8,128,128]{3,2,1,0:T(8,128)} %param.6), kind=kOutput, calls=%fused_computation.30 | convolution fusion | flops 1610612736 | bytes 8912896 | tf_op jit(solution)/shard_map/iknm,ikmc->inc/dot_general | solution.py:52
  375.6 140.5 %all-reduce.6.cloned.1.call-done = f32[128,128]{0,1:T(8,128)} async-done(((f32[128,128]{0,1:T(8,128)}), f32[128,128]{0,1:T(8,128)}) %all-reduce.6.cloned.1.call-update) | async-done | bytes 65552 | tf_op jit(solution)/shard_map/psum | solution.py:98
  (56 shorter events, 36.2 us)
Async XLA Ops:
  7.2 1.5 copy-start
  7.2 164.5 %all-gather.2.cloned.1.call-start = ((), (), s32[]{:S(2)}) async-start(), calls=%async_computation | async-start | bytes 4718592 | tf_op jit(solution)/shard_map/all_gather | solution.py:92
  8.6 10.3 %copy-start.3 = (s32[8,8]{1,0:T(8,128)S(1)}, s32[8,8]{1,0:T(8,128)}, u32[]{:S(2)}) copy-start(s32[8,8]{1,0:T(8,128)} %param.5) | copy-start | bytes 772
  10.3 9.9 %copy-start.2 = (f32[8,128]{1,0:T(8,128)S(1)}, f32[8,128]{1,0:T(8,128)}, u32[]{:S(2)}) copy-start(f32[8,128]{1,0:T(8,128)} %param.8) | copy-start | bytes 12292
  12.9 26.5 %collective-permute-start = (f32[1024,256]{1,0:T(8,128)}, f32[1024,256]{1,0:T(8,128)}, u32[]{:S(2)}, u32[]{:S(2)}) collective-permute-start(f32[1024,256]{1,0:T(8,128)} %bitcast.3), channel_id=1, source_target_pairs={{0,1},{1,2},{2,3},{3,4},{4,5},{5,6},{6,7},{7,8},{8,9},{9,10},{10,1... | collective-permute-start | bytes 3145736 | tf_op jit(solution)/shard_map/ppermute | solution.py:16
  17.7 26.8 %collective-permute-start.1 = (f32[1024,256]{1,0:T(8,128)}, f32[1024,256]{1,0:T(8,128)}, u32[]{:S(2)}, u32[]{:S(2)}) collective-permute-start(f32[1024,256]{1,0:T(8,128)} %bitcast.3), channel_id=1, source_target_pairs={{1,0},{2,1},{3,2},{4,3},{5,4},{6,5},{7,6},{8,7},{9,8},{10,9},{11,1... | collective-permute-start | bytes 3145736 | tf_op jit(solution)/shard_map/ppermute | solution.py:19
  75.8 24.8 %collective-permute-start.2 = (f32[1024,256]{1,0:T(8,128)}, f32[1024,256]{1,0:T(8,128)}, u32[]{:S(2)}, u32[]{:S(2)}) collective-permute-start(f32[1024,256]{1,0:T(8,128)} %bitcast.11), channel_id=1, source_target_pairs={{0,1},{1,2},{2,3},{3,4},{4,5},{5,6},{6,7},{7,8},{8,9},{9,10},{10,1... | collective-permute-start | bytes 3145736 | tf_op jit(solution)/shard_map/ppermute | solution.py:16
  79.8 26.4 %collective-permute-start.3 = (f32[1024,256]{1,0:T(8,128)}, f32[1024,256]{1,0:T(8,128)}, u32[]{:S(2)}, u32[]{:S(2)}) collective-permute-start(f32[1024,256]{1,0:T(8,128)} %bitcast.11), channel_id=1, source_target_pairs={{1,0},{2,1},{3,2},{4,3},{5,4},{6,5},{7,6},{8,7},{9,8},{10,9},{11,1... | collective-permute-start | bytes 3145736 | tf_op jit(solution)/shard_map/ppermute | solution.py:19
  136.9 181.2 %all-reduce.4.cloned.1.call-start = ((), (), s32[]{:S(2)}) async-start(), calls=%async_computation.1 | async-start | bytes 131072 | tf_op jit(solution)/shard_map/psum | solution.py:93
  175.8 340.4 %all-reduce.6.cloned.1.call-start = ((), (), s32[]{:S(2)}) async-start(), calls=%async_computation.2 | async-start | bytes 131072 | tf_op jit(solution)/shard_map/psum | solution.py:98
  343.5 10.1 %collective-permute-start.4 = (f32[1024,128]{0,1:T(8,128)S(1)}, f32[1024,128]{0,1:T(8,128)S(1)}, u32[]{:S(2)}, u32[]{:S(2)}) collective-permute-start(f32[1024,128]{0,1:T(8,128)S(1)} %bitcast.115), channel_id=1, source_target_pairs={{0,1},{1,2},{2,3},{3,4},{4,5},{5,6},{6,7},{7,8},{8,9},{9,10},{10,1... | collective-permute-start | bytes 1572872 | tf_op jit(solution)/shard_map/ppermute | solution.py:16
  346.7 11.1 %collective-permute-start.5 = (f32[1024,128]{0,1:T(8,128)S(1)}, f32[1024,128]{0,1:T(8,128)S(1)}, u32[]{:S(2)}, u32[]{:S(2)}) collective-permute-start(f32[1024,128]{0,1:T(8,128)S(1)} %bitcast.116), channel_id=1, source_target_pairs={{1,0},{2,1},{3,2},{4,3},{5,4},{6,5},{7,6},{8,7},{9,8},{10,9},{11,1... | collective-permute-start | bytes 1572872 | tf_op jit(solution)/shard_map/ppermute | solution.py:19
  373.0 144.7 %copy-start.1 = (f32[8,128,128]{1,2,0:T(8,128)}, f32[8,128,128]{1,2,0:T(8,128)S(1)}, u32[]{:S(2)}) copy-start(f32[8,128,128]{1,2,0:T(8,128)S(1)} %convolution_add_fusion) | copy-start | bytes 1572868
Sparse Core Ops, SparseCore 0:
  137.1 34.5 all-gather.1
  175.9 142.2 all-reduce.3
  374.7 141.3 all-reduce.5
